TPU v7x, 32 devices: a whole 2x2x4 slice. The times are simulated.
32 devices in a mesh: rep: 2 (over x), seq: 16 (over z, y, core).
Axes of the slice: x: 2, y: 2, z: 4, core: 2. Of those that a mesh axis runs over, the one named last changes fastest.
Arguments:
- projected: bfloat16 [24576, 4096], P(('rep', 'seq')), parts along dimension 0, may hold values from -6 to 6
- history_in: bfloat16 [24576, 1024], P(('rep', 'seq')), parts along dimension 0, may hold values from -6 to 6
- norm_gain: float32 [1024], replicated, may hold values from 0.1 to 1.9
- out_proj: bfloat16 [1024, 1024], replicated, may hold values from -0.1875 to 0.1875
- user_spans: int32 [16], P('rep'), parts along dimension 0, may hold values from 1 to 4, as said below
- user_tails: int32 [16], P('rep'), parts along dimension 0, may hold values from 1 to 768
- cand_emb: bfloat16 [4096, 1024], P(('rep', 'seq')), parts along dimension 0, may hold values from -6 to 6
- cand_user: int32 [4096], P(('rep', 'seq')), parts along dimension 0, may hold values from 0 to 7
- cross_down: bfloat16 [2048, 128], replicated, may hold values from -0.125 to 0.125
- cross_up: bfloat16 [128, 2048], replicated, may hold values from -0.5 to 0.5
- cross_bias: float32 [2048], replicated, may hold values from -4 to 4
- score_weight: float32 [2048], replicated, may hold values from -0.125 to 0.125
Outputs:
- history_out: bfloat16 [24576, 1024], P(('rep', 'seq')), parts along dimension 0
- scores: float32 [4096], P(('rep', 'seq')), parts along dimension 0
There are 2 independent parts, one for each index of `rep`. A program takes and returns all parts, laid end to end along the dimension named above; an argument that names none is the same for every part. Nothing has to cross between parts.
Inputs may be any that keep to these rules, and one draw needn't show every extreme that they name: `user_spans`: users own consecutive segments in order and together own all 16 segments; some user owns exactly 4.
All inputs are finite; a program needn't handle non-finite values.
Results may differ from a plain program's by a relative error of at most 0.0059.
Values may be sent and summed in bfloat16 or wider, within the bound.
A program may use at most 128 MiB of HBM per device.

v0:
```python
import jax
import jax.numpy as jnp
from jax import lax
from jax.sharding import PartitionSpec as P

HEADS = 8


def shifted(x, axis, by):
    peers = lax.axis_size(axis)
    pairs = [(i, i + by) for i in range(peers) if 0 <= i + by < peers]
    return lax.ppermute(x, axis, pairs)


def attend(totals, queries, key_values, weight_mask, score_scale):
    key_count = key_values.shape[0]
    model_width = key_values.shape[1] // 2
    head_count = queries.shape[1]
    key_part = key_values[:, :model_width].reshape(key_count, head_count, -1)
    value_part = key_values[:, model_width:].reshape(key_count, head_count, -1)
    logits = (
        jnp.einsum("qhd,khd->hqk", queries, key_part, preferred_element_type=jnp.float32)
        * score_scale
    )
    weights = (jax.nn.silu(logits) * weight_mask).astype(jnp.bfloat16)
    return totals + jnp.einsum(
        "hqk,khd->qhd", weights, value_part, preferred_element_type=jnp.float32
    )


def body(
    projected,
    history_in,
    norm_gain,
    out_proj,
    user_spans,
    user_tails,
    cand_emb,
    cand_user,
    cross_down,
    cross_up,
    cross_bias,
    score_weight,
):
    row_count, model_width = history_in.shape
    head_size = model_width // HEADS
    score_scale = head_size ** (-0.5)
    devices = lax.axis_size("seq")
    my_index = lax.axis_index("seq")
    span_limit = min(4, devices // 2)
    last_dev = jnp.cumsum(user_spans) - 1
    first_dev = last_dev - user_spans + 1
    device_ids = jnp.arange(devices, dtype=jnp.int32)
    owner_of = jnp.sum((first_dev[None, :] <= device_ids[:, None]).astype(jnp.int32), axis=1) - 1
    is_end = device_ids == last_dev[owner_of]
    valid_rows = jnp.where(is_end, user_tails[owner_of], row_count)
    queries = projected[:, model_width : 2 * model_width].reshape(row_count, HEADS, head_size)
    own_block = projected[:, 2 * model_width :]
    row_ids = jnp.arange(row_count, dtype=jnp.int32)
    causal = (row_ids[None, :] <= row_ids[:, None]).astype(jnp.float32)
    totals = attend(
        jnp.zeros((row_count, HEADS, head_size), jnp.float32),
        queries,
        own_block,
        causal,
        score_scale,
    )

    def add_block(totals, key_values, offset):
        source = my_index - offset
        same_user = (source >= 0) & (owner_of[jnp.maximum(source, 0)] == owner_of[my_index])
        result = lax.cond(
            same_user,
            lambda current: attend(current, queries, key_values, jnp.float32(1.0), score_scale),
            lambda current: current,
            totals,
        )
        return result

    def next_block(offset, loop_state):
        totals, moving = loop_state
        moving = shifted(moving, "seq", 1)
        return (add_block(totals, moving, offset), moving)

    totals, moving = lax.fori_loop(1, span_limit, next_block, (totals, own_block))
    valid_here = valid_rows[my_index]
    row_valid = (row_ids < valid_here).astype(jnp.float32)
    attention = totals.reshape(row_count, model_width) * row_valid[:, None]
    row_mean = jnp.mean(attention, axis=1, keepdims=True)
    centered = attention - row_mean
    row_var = jnp.mean(centered * centered, axis=1, keepdims=True)
    normed = centered * lax.rsqrt(row_var + 1e-06) * norm_gain
    gated = (normed * projected[:, :model_width].astype(jnp.float32)).astype(jnp.bfloat16)
    history_out = (
        jnp.dot(gated, out_proj, preferred_element_type=jnp.float32)
        + history_in.astype(jnp.float32)
    ).astype(jnp.bfloat16)
    last_row = jnp.where(is_end[my_index], valid_here - 1, 0)
    final_row = lax.dynamic_slice_in_dim(history_out, last_row, 1, 0)
    final_row = jnp.where(is_end[my_index], final_row, jnp.zeros_like(final_row))
    user_rows = lax.all_gather(final_row, "seq", axis=0, tiled=True)
    user_count = user_spans.shape[0]
    user_match = cand_user[:, None] == jnp.arange(user_count, dtype=jnp.int32)[None, :]
    cand_dev = jnp.sum(jnp.where(user_match, last_dev[None, :], 0), axis=1)
    selector = (cand_dev[:, None] == device_ids[None, :]).astype(jnp.bfloat16)
    user_part = jnp.dot(selector, user_rows, preferred_element_type=jnp.float32).astype(
        jnp.bfloat16
    )
    crossed_in = jnp.concatenate([user_part, cand_emb], axis=1)
    low_rank = jnp.dot(crossed_in, cross_down, preferred_element_type=jnp.float32).astype(
        jnp.bfloat16
    )
    up_part = jnp.dot(low_rank, cross_up, preferred_element_type=jnp.float32)
    input_float = crossed_in.astype(jnp.float32)
    crossed = input_float * (up_part + cross_bias) + input_float
    scores = jnp.sum(crossed * score_weight, axis=1)
    return (history_out, scores)


def solution(mesh):
    in_specs = (
        P(("rep", "seq"), None),
        P(("rep", "seq"), None),
        P(),
        P(),
        P("rep"),
        P("rep"),
        P(("rep", "seq"), None),
        P(("rep", "seq")),
        P(),
        P(),
        P(),
        P(),
    )
    out_specs = (P(("rep", "seq"), None), P(("rep", "seq")))
    return jax.shard_map(body, mesh=mesh, in_specs=in_specs, out_specs=out_specs, check_vma=False)
```

profile of v0, /device:TPU:7, one launch (start us, length us, event | category | flops | bytes accessed | tf_op | source)
XLA Modules:
  0.0 261.3 jit_solution(10896016889106156357)
XLA Ops:
  3.5 5.7 %fusion.36 = (bf16[768,1024]{1,0:T(8,128)(2,1)}, bf16[768,1024]{1,0:T(8,128)(2,1)}, bf16[768,1024]{1,0:T(8,128)(2,1)}, bf16[768,1024]{1,0:T(8,128)(2,1)}) fusion(bf16[768,4096]{1,0:T(8,128)(2,1)} %param.16), kind=kLoop, calls=%fused_computation.59 | loop fusion | bytes 12582912 | tf_op jit(solution)/shard_map/slice | solution.py:93
  9.2 2.6 copy.56
  11.8 2.7 %copy.57 = bf16[768,1024]{0,1:T(8,128)(2,1)} copy(bf16[768,1024]{1,0:T(8,128)(2,1)} %get-tuple-element.218) | data formatting | bytes 3145728
  14.4 2.6 copy.58
  18.6 12.1 %fusion.17 = f32[768,8,128]{2,0,1:T(8,128)} fusion(bf16[768,8,128]{0,2,1:T(8,128)(2,1)} %bitcast.57, f32[768,768]{1,0:T(8,128)} %fusion.16, bf16[768,8,128]{0,2,1:T(8,128)(2,1)} %bitcast.54, bf16[768,8,128]{0,2,1:T(8,128)(2,1)} %bitcast.56), kind=kOutput, calls=%fused_computation.26 | convolution fusion | flops 2448949248 | bytes 10223616 | tf_op jit(solution)/shard_map/hqk,khd->qhd/dot_general | solution.py:26
  30.7 2.6 copy.47
  33.3 4.0 %slice.26 = bf16[768,2048]{1,0:T(8,128)(2,1)} slice(bf16[768,4096]{1,0:T(8,128)(2,1)} %param.16), slice={[0:768], [2048:4096]} | slice | bytes 6291456 | tf_op jit(solution)/shard_map/slice | solution.py:58
  37.2 4.7 %copy.59 = bf16[768,2048]{0,1:T(8,128)(2,1)} copy(bf16[768,2048]{1,0:T(8,128)(2,1)} %slice.26) | data formatting | bytes 6291456
  42.0 129.2 %while.20 = (s32[]{:T(128)}, f32[768,8,128]{2,0,1:T(8,128)}, bf16[768,2048]{0,1:T(8,128)(2,1)}, s32[]{:T(128)}, s32[16]{0:T(128)S(1)}, /*index=5*/s32[1]{0:T(128)}, bf16[768,8,128]{2,0,1:T(8,128)(2,1)}, s32[]{:T(128)}, s32[]{:T(128)}) while((s32[]{:T(128)}, f32[768,8,128]{2,0,1:T(8,128)}, bf16[768,2048]{0,1:T(8,128)(2,1)}, s32[]{:T(128)}, ...), condition=%wide.region_5.6_spmd, body=%wide.region_2.5_spmd.sunk | while | flops 2445017088 | bytes 36176096 | solution.py:85
  42.0 3.7 %collective-permute-start = (bf16[768,2048]{0,1:T(8,128)(2,1)}, bf16[768,2048]{0,1:T(8,128)(2,1)}, u32[]{:S(2)}, u32[]{:S(2)}) collective-permute-start(bf16[768,2048]{0,1:T(8,128)(2,1)} %get-tuple-element.274), channel_id=1, source_target_pairs={{0,1},{1,2},{2,3},{3,4},{4,5},{5,6},{6,7},{7,8},{8,9},{9,10},{10,1... | collective-permute-start | bytes 9437192 | tf_op jit(solution)/shard_map/while/body/eval_jaxpr/ppermute | solution.py:12
  47.5 32.7 %collective-permute-done = bf16[768,2048]{0,1:T(8,128)(2,1)} collective-permute-done((bf16[768,2048]{0,1:T(8,128)(2,1)}, bf16[768,2048]{0,1:T(8,128)(2,1)}, u32[]{:S(2)}, u32[]{:S(2)}) %collective-permute-start) | collective-permute-done | bytes 3145760 | tf_op jit(solution)/shard_map/while/body/eval_jaxpr/ppermute | solution.py:12
  80.2 3.8 %copy.75 = bf16[768,2048]{0,1:T(8,128)(2,1)} copy(bf16[768,2048]{0,1:T(8,128)(2,1)} %collective-permute-done) | data formatting | bytes 6291456 | tf_op jit(solution)/shard_map/while
  84.0 5.3 %collective-permute-start = (bf16[768,2048]{0,1:T(8,128)(2,1)}, bf16[768,2048]{0,1:T(8,128)(2,1)}, u32[]{:S(2)}, u32[]{:S(2)}) collective-permute-start(bf16[768,2048]{0,1:T(8,128)(2,1)} %get-tuple-element.274), channel_id=1, source_target_pairs={{0,1},{1,2},{2,3},{3,4},{4,5},{5,6},{6,7},{7,8},{8,9},{9,10},{10,1... | collective-permute-start | bytes 9437192 | tf_op jit(solution)/shard_map/while/body/eval_jaxpr/ppermute | solution.py:12
  91.1 32.7 %collective-permute-done = bf16[768,2048]{0,1:T(8,128)(2,1)} collective-permute-done((bf16[768,2048]{0,1:T(8,128)(2,1)}, bf16[768,2048]{0,1:T(8,128)(2,1)}, u32[]{:S(2)}, u32[]{:S(2)}) %collective-permute-start) | collective-permute-done | bytes 3145760 | tf_op jit(solution)/shard_map/while/body/eval_jaxpr/ppermute | solution.py:12
  123.8 3.8 %copy.75 = bf16[768,2048]{0,1:T(8,128)(2,1)} copy(bf16[768,2048]{0,1:T(8,128)(2,1)} %collective-permute-done) | data formatting | bytes 6291456 | tf_op jit(solution)/shard_map/while
  127.6 5.3 %collective-permute-start = (bf16[768,2048]{0,1:T(8,128)(2,1)}, bf16[768,2048]{0,1:T(8,128)(2,1)}, u32[]{:S(2)}, u32[]{:S(2)}) collective-permute-start(bf16[768,2048]{0,1:T(8,128)(2,1)} %get-tuple-element.274), channel_id=1, source_target_pairs={{0,1},{1,2},{2,3},{3,4},{4,5},{5,6},{6,7},{7,8},{8,9},{9,10},{10,1... | collective-permute-start | bytes 9437192 | tf_op jit(solution)/shard_map/while/body/eval_jaxpr/ppermute | solution.py:12
  134.7 32.7 %collective-permute-done = bf16[768,2048]{0,1:T(8,128)(2,1)} collective-permute-done((bf16[768,2048]{0,1:T(8,128)(2,1)}, bf16[768,2048]{0,1:T(8,128)(2,1)}, u32[]{:S(2)}, u32[]{:S(2)}) %collective-permute-start) | collective-permute-done | bytes 3145760 | tf_op jit(solution)/shard_map/while/body/eval_jaxpr/ppermute | solution.py:12
  167.4 3.8 %copy.75 = bf16[768,2048]{0,1:T(8,128)(2,1)} copy(bf16[768,2048]{0,1:T(8,128)(2,1)} %collective-permute-done) | data formatting | bytes 6291456 | tf_op jit(solution)/shard_map/while
  177.0 3.7 %copy.48 = f32[768,8,128]{0,2,1:T(8,128)} copy(f32[768,8,128]{2,0,1:T(8,128)} %get-tuple-element.178) | data formatting | bytes 6291456 | tf_op jit(solution)/shard_map/while | solution.py:85
  180.7 2.6 copy.60
  183.3 3.2 %fusion.12 = bf16[768,1024]{0,1:T(8,128)(2,1)S(1)} fusion(f32[768,8,128]{0,2,1:T(8,128)} %copy.48, bf16[768,1024]{0,1:T(8,128)(2,1)} %copy.60, f32[1024]{0:T(1024)S(1)} %copy-done.3, f32[768]{0:T(1024)S(1)} %add_rsqrt_fusion, f32[768]{0:T(1024)S(1)} %broadcast_multiply_fusion, f32[768]{0:T(1024)S(1)} %fusion.29), kind=kLoop, calls=%fused_computation.16 | loop fusion | flops 5505024 | bytes 6304768 | tf_op jit(solution)/shard_map/convert_element_type | solution.py:93
  186.5 3.0 %add_convert_fusion = bf16[768,1024]{1,0:T(8,128)(2,1)} fusion(bf16[768,1024]{1,0:T(8,128)(2,1)S(1)} %copy-done.4, bf16[768,1024]{0,1:T(8,128)(2,1)S(1)} %fusion.12, bf16[1024,1024]{1,0:T(8,128)(2,1)S(1)} %copy-done), kind=kOutput, calls=%fused_computation.17 | convolution fusion | flops 1612972032 | bytes 6815744 | tf_op jit(solution)/shard_map/dot_general | solution.py:95
  192.8 65.8 %all-gather = bf16[16,1,1024]{2,1,0:T(2,128)(2,1)S(1)} all-gather(bf16[1,1,1024]{2,1,0:T(2,128)(2,1)S(1)} %fusion.28), channel_id=1, replica_groups=mesh['rep'=2,'seq'=16] {'seq'}, dimensions={0}, use_global_device_ids=true | all-gather | bytes 34816 | tf_op jit(solution)/shard_map/all_gather | solution.py:101
  259.0 2.3 fusion.18
  (57 shorter events, 14.3 us)
Async XLA Ops:
  0.6 185.8 %copy-start = (bf16[1024,1024]{1,0:T(8,128)(2,1)S(1)}, bf16[1024,1024]{1,0:T(8,128)(2,1)}, u32[]{:S(2)}) copy-start(bf16[1024,1024]{1,0:T(8,128)(2,1)} %param.19) | copy-start | bytes 6291460
  1.6 7.5 %copy-start.10 = (s32[8,1]{0,1:T(1,128)}, s32[8,1]{0,1:T(1,128)S(1)}, u32[]{:S(2)}) copy-start(s32[8,1]{0,1:T(1,128)S(1)} %reduce-window.7) | copy-start | bytes 100
  2.4 0.5 copy-start.12
  42.0 129.2 %copy-start.13 = (s32[16]{0:T(128)S(1)}, s32[16]{0:T(128)}, u32[]{:S(2)}) copy-start(s32[16]{0:T(128)} %copy-done.12) | copy-start | bytes 196
  42.0 129.2 %copy-start.11 = (s32[8,1]{0,1:T(1,128)S(1)}, s32[8,1]{0,1:T(1,128)}, u32[]{:S(2)}) copy-start(s32[8,1]{0,1:T(1,128)} %copy-done.10) | copy-start | bytes 100
  42.0 129.9 %copy-start.1 = (s32[8]{0:T(128)S(1)}, s32[8]{0:T(128)}, u32[]{:S(2)}) copy-start(s32[8]{0:T(128)} %param.21) | copy-start | bytes 100
  42.0 38.2 %collective-permute-start = (bf16[768,2048]{0,1:T(8,128)(2,1)}, bf16[768,2048]{0,1:T(8,128)(2,1)}, u32[]{:S(2)}, u32[]{:S(2)}) collective-permute-start(bf16[768,2048]{0,1:T(8,128)(2,1)} %get-tuple-element.274), channel_id=1, source_target_pairs={{0,1},{1,2},{2,3},{3,4},{4,5},{5,6},{6,7},{7,8},{8,9},{9,10},{10,1... | collective-permute-start | bytes 9437192 | tf_op jit(solution)/shard_map/while/body/eval_jaxpr/ppermute | solution.py:12
  84.0 39.8 %collective-permute-start = (bf16[768,2048]{0,1:T(8,128)(2,1)}, bf16[768,2048]{0,1:T(8,128)(2,1)}, u32[]{:S(2)}, u32[]{:S(2)}) collective-permute-start(bf16[768,2048]{0,1:T(8,128)(2,1)} %get-tuple-element.274), channel_id=1, source_target_pairs={{0,1},{1,2},{2,3},{3,4},{4,5},{5,6},{6,7},{7,8},{8,9},{9,10},{10,1... | collective-permute-start | bytes 9437192 | tf_op jit(solution)/shard_map/while/body/eval_jaxpr/ppermute | solution.py:12
  127.6 39.8 %collective-permute-start = (bf16[768,2048]{0,1:T(8,128)(2,1)}, bf16[768,2048]{0,1:T(8,128)(2,1)}, u32[]{:S(2)}, u32[]{:S(2)}) collective-permute-start(bf16[768,2048]{0,1:T(8,128)(2,1)} %get-tuple-element.274), channel_id=1, source_target_pairs={{0,1},{1,2},{2,3},{3,4},{4,5},{5,6},{6,7},{7,8},{8,9},{9,10},{10,1... | collective-permute-start | bytes 9437192 | tf_op jit(solution)/shard_map/while/body/eval_jaxpr/ppermute | solution.py:12
  172.5 3.8 %copy-start.2 = (f32[768,8,128]{2,0,1:T(8,128)S(1)}, f32[768,8,128]{2,0,1:T(8,128)}, u32[]{:S(2)}) copy-start(f32[768,8,128]{2,0,1:T(8,128)} %get-tuple-element.178) | copy-start | bytes 9437188
  180.7 2.6 copy-start.3
  183.3 3.2 %copy-start.4 = (bf16[768,1024]{1,0:T(8,128)(2,1)S(1)}, bf16[768,1024]{1,0:T(8,128)(2,1)}, u32[]{:S(2)}) copy-start(bf16[768,1024]{1,0:T(8,128)(2,1)} %param.17) | copy-start | bytes 4718596
  186.5 72.1 %copy-start.9 = (s32[128]{0:T(128)S(1)}, s32[128]{0:T(128)}, u32[]{:S(2)}) copy-start(s32[128]{0:T(128)} %param.23) | copy-start | bytes 1540
  186.5 72.5 %copy-start.5 = (bf16[128,2048]{1,0:T(8,128)(2,1)S(1)}, bf16[128,2048]{1,0:T(8,128)(2,1)}, u32[]{:S(2)}) copy-start(bf16[128,2048]{1,0:T(8,128)(2,1)} %param.25) | copy-start | bytes 1572868
  186.5 72.5 %copy-start.6 = (bf16[2048,128]{1,0:T(8,128)(2,1)S(1)}, bf16[2048,128]{1,0:T(8,128)(2,1)}, u32[]{:S(2)}) copy-start(bf16[2048,128]{1,0:T(8,128)(2,1)} %param.24) | copy-start | bytes 1572868
  186.5 72.5 %copy-start.7 = (f32[2048]{0:T(1024)S(1)}, f32[2048]{0:T(1024)}, u32[]{:S(2)}) copy-start(f32[2048]{0:T(1024)} %param.27) | copy-start | bytes 24580
  186.5 72.5 %copy-start.8 = (f32[2048]{0:T(1024)S(1)}, f32[2048]{0:T(1024)}, u32[]{:S(2)}) copy-start(f32[2048]{0:T(1024)} %param.26) | copy-start | bytes 24580
where the time goes:
time: 262 us; the launch traced here: 261 us
  waiting for transfers between devices  98 us (37%)
  blocking collectives  65.8 us (25%)
  local copies, waits for them, and re-layouts  48 us (18%)
  matrix products  17.6 us (7%)
  starting transfers between devices  14.3 us (5%)
  other arithmetic  11.7 us (4%)
  loops' own time  3.68 us (1%)
    ppermute x3, waiting for transfers between devices, shifted(): return lax.ppermute(x, axis, pairs)  98 us
    all_gather x1, blocking collectives, body(): user_rows = lax.all_gather(final_row, 'seq', axis=0, tiled=True)  65.8 us
    unnamed x33, local copies, waits for them, and re-layouts  15.8 us
    ppermute x3, starting transfers between devices, shifted(): return lax.ppermute(x, axis, pairs)  14.3 us
    dot_general x1, matrix products, attend(): jnp.einsum('hqk,khd->qhd', weights, value_part, preferred_element_type=jn...  12.1 us
    while x3, local copies, waits for them, and re-layouts  11.4 us
    while x2, local copies, waits for them, and re-layouts, body(): lax.fori_loop(1, span_limit, next_block, (totals, own_block))  6.32 us
    slice x1, local copies, waits for them, and re-layouts, body(): projected[:, :model_width].astype(jnp.float32)  5.67 us
  transfers between devices with their start and end apart: 3, of which 3 were waited for; matrix products, arithmetic and copies ran while one was open for 1% of the time, Pallas kernels for 0%

commit v1 on v0

--- a/solution.py
+++ b/solution.py
@@ -98,7 +98,10 @@
     last_row = jnp.where(is_end[my_index], valid_here - 1, 0)
     final_row = lax.dynamic_slice_in_dim(history_out, last_row, 1, 0)
     final_row = jnp.where(is_end[my_index], final_row, jnp.zeros_like(final_row))
-    user_rows = lax.all_gather(final_row, "seq", axis=0, tiled=True)
+    count = lax.axis_size("seq")
+    parts = jnp.stack([final_row for _ in range(count)])
+    parts = lax.all_to_all(parts, "seq", split_axis=0, concat_axis=0)
+    user_rows = jnp.concatenate(parts, axis=0)
     user_count = user_spans.shape[0]
     user_match = cand_user[:, None] == jnp.arange(user_count, dtype=jnp.int32)[None, :]
     cand_dev = jnp.sum(jnp.where(user_match, last_dev[None, :], 0), axis=1)

time: 262 us -> 254 us (0.969)
  blocking collectives: 65.8 us -> 0 us
  starting transfers between devices: 14.3 us -> 66.9 us
  waiting for transfers between devices: 98 us -> 103 us
    all_gather x1 -> x0, blocking collectives: 65.8 us -> none  [body(): user_rows = lax.all_gather(final_row, 'seq', axis=0, tiled=True)]
    all_to_all x0 -> x1, starting transfers between devices: none -> 52.7 us  [body(): parts = lax.all_to_all(parts, 'seq', split_axis=0, concat_axis=0)]
    all_to_all x0 -> x1, waiting for transfers between devices: none -> 4.95 us  [body(): parts = lax.all_to_all(parts, 'seq', split_axis=0, concat_axis=0)]
    unnamed x33 -> x43, local copies, waits for them, and re-layouts: 15.8 us -> 17.6 us
  transfers between devices with their start and end apart: 3 -> 4, of which waited for: 3 -> 4; matrix products, arithmetic and copies ran while one was open for 1% -> 1% of each run, Pallas kernels for 0% -> 0%
where the time goes in v1:
time: 254 us; the launch traced here: 252 us
  waiting for transfers between devices  103 us (41%)
  starting transfers between devices  66.9 us (26%)
  local copies, waits for them, and re-layouts  48.7 us (19%)
  matrix products  16.5 us (6%)
  other arithmetic  11.3 us (4%)
  loops' own time  3.91 us (2%)
    ppermute x3, waiting for transfers between devices, shifted(): return lax.ppermute(x, axis, pairs)  97.8 us
    all_to_all x1, starting transfers between devices, body(): parts = lax.all_to_all(parts, 'seq', split_axis=0, concat_axis=0)  52.7 us
    unnamed x43, local copies, waits for them, and re-layouts  17.6 us
    ppermute x3, starting transfers between devices, shifted(): return lax.ppermute(x, axis, pairs)  14.3 us
    dot_general x1, matrix products, attend(): jnp.einsum('hqk,khd->qhd', weights, value_part, preferred_element_type=jn...  12.1 us
    while x3, local copies, waits for them, and re-layouts  11.2 us
    slice x1, local copies, waits for them, and re-layouts, body(): projected[:, :model_width].astype(jnp.float32)  6.45 us
    while x2, local copies, waits for them, and re-layouts, body(): lax.fori_loop(1, span_limit, next_block, (totals, own_block))  6.09 us
  transfers between devices with their start and end apart: 4, of which 4 were waited for; matrix products, arithmetic and copies ran while one was open for 1% of the time, Pallas kernels for 0%

profile of v1, /device:TPU:7, one launch (start us, length us, event | category | flops | bytes accessed | tf_op | source)
XLA Modules:
  0.0 252.2 jit_solution(243588154979931169)
XLA Ops:
  2.3 6.5 %fusion.36 = (bf16[768,1024]{1,0:T(8,128)(2,1)}, bf16[768,1024]{1,0:T(8,128)(2,1)}, bf16[768,1024]{1,0:T(8,128)(2,1)}, bf16[768,1024]{1,0:T(8,128)(2,1)}) fusion(bf16[768,4096]{1,0:T(8,128)(2,1)} %param.16), kind=kLoop, calls=%fused_computation.59 | loop fusion | bytes 12582912 | tf_op jit(solution)/shard_map/slice | solution.py:93
  11.0 2.6 %copy.56 = bf16[768,1024]{0,1:T(8,128)(2,1)} copy(bf16[768,1024]{1,0:T(8,128)(2,1)} %get-tuple-element.219) | data formatting | bytes 3145728
  13.6 2.6 %copy.57 = bf16[768,1024]{0,1:T(8,128)(2,1)} copy(bf16[768,1024]{1,0:T(8,128)(2,1)} %get-tuple-element.218) | data formatting | bytes 3145728
  16.2 2.6 %copy.58 = bf16[768,1024]{0,1:T(8,128)(2,1)} copy(bf16[768,1024]{1,0:T(8,128)(2,1)} %get-tuple-element.217) | data formatting | bytes 3145728
  18.8 2.6 %copy.47 = bf16[768,8,128]{2,0,1:T(8,128)(2,1)} copy(bf16[768,8,128]{0,2,1:T(8,128)(2,1)} %bitcast.54) | data formatting | bytes 3145728 | tf_op jit(solution)/shard_map/while | solution.py:85
  21.4 4.6 %copy.59 = bf16[768,2048]{0,1:T(8,128)(2,1)} copy(bf16[768,2048]{1,0:T(8,128)(2,1)} %slice.26) | data formatting | bytes 6291456
  30.2 12.1 %fusion.17 = f32[768,8,128]{2,0,1:T(8,128)} fusion(bf16[768,8,128]{0,2,1:T(8,128)(2,1)} %bitcast.57, f32[768,768]{1,0:T(8,128)} %fusion.16, bf16[768,8,128]{0,2,1:T(8,128)(2,1)} %bitcast.55, bf16[768,8,128]{0,2,1:T(8,128)(2,1)} %bitcast.56), kind=kOutput, calls=%fused_computation.26 | convolution fusion | flops 2448949248 | bytes 10223616 | tf_op jit(solution)/shard_map/hqk,khd->qhd/dot_general | solution.py:26
  42.3 129.0 %while.20 = (s32[]{:T(128)}, f32[768,8,128]{2,0,1:T(8,128)}, bf16[768,2048]{0,1:T(8,128)(2,1)}, s32[]{:T(128)}, s32[16]{0:T(128)S(1)}, /*index=5*/s32[1]{0:T(128)}, bf16[768,8,128]{2,0,1:T(8,128)(2,1)}, s32[]{:T(128)}, s32[]{:T(128)}) while((s32[]{:T(128)}, f32[768,8,128]{2,0,1:T(8,128)}, bf16[768,2048]{0,1:T(8,128)(2,1)}, s32[]{:T(128)}, ...), condition=%wide.region_5.6_spmd, body=%wide.region_2.5_spmd.sunk | while | flops 2445017088 | bytes 36176096 | solution.py:85
  42.3 3.7 %collective-permute-start = (bf16[768,2048]{0,1:T(8,128)(2,1)}, bf16[768,2048]{0,1:T(8,128)(2,1)}, u32[]{:S(2)}, u32[]{:S(2)}) collective-permute-start(bf16[768,2048]{0,1:T(8,128)(2,1)} %get-tuple-element.274), channel_id=1, source_target_pairs={{0,1},{1,2},{2,3},{3,4},{4,5},{5,6},{6,7},{7,8},{8,9},{9,10},{10,1... | collective-permute-start | bytes 9437192 | tf_op jit(solution)/shard_map/while/body/eval_jaxpr/ppermute | solution.py:12
  47.9 32.6 %collective-permute-done = bf16[768,2048]{0,1:T(8,128)(2,1)} collective-permute-done((bf16[768,2048]{0,1:T(8,128)(2,1)}, bf16[768,2048]{0,1:T(8,128)(2,1)}, u32[]{:S(2)}, u32[]{:S(2)}) %collective-permute-start) | collective-permute-done | bytes 3145760 | tf_op jit(solution)/shard_map/while/body/eval_jaxpr/ppermute | solution.py:12
  80.5 3.7 %copy.75 = bf16[768,2048]{0,1:T(8,128)(2,1)} copy(bf16[768,2048]{0,1:T(8,128)(2,1)} %collective-permute-done) | data formatting | bytes 6291456 | tf_op jit(solution)/shard_map/while
  84.3 5.3 %collective-permute-start = (bf16[768,2048]{0,1:T(8,128)(2,1)}, bf16[768,2048]{0,1:T(8,128)(2,1)}, u32[]{:S(2)}, u32[]{:S(2)}) collective-permute-start(bf16[768,2048]{0,1:T(8,128)(2,1)} %get-tuple-element.274), channel_id=1, source_target_pairs={{0,1},{1,2},{2,3},{3,4},{4,5},{5,6},{6,7},{7,8},{8,9},{9,10},{10,1... | collective-permute-start | bytes 9437192 | tf_op jit(solution)/shard_map/while/body/eval_jaxpr/ppermute | solution.py:12
  91.5 32.6 %collective-permute-done = bf16[768,2048]{0,1:T(8,128)(2,1)} collective-permute-done((bf16[768,2048]{0,1:T(8,128)(2,1)}, bf16[768,2048]{0,1:T(8,128)(2,1)}, u32[]{:S(2)}, u32[]{:S(2)}) %collective-permute-start) | collective-permute-done | bytes 3145760 | tf_op jit(solution)/shard_map/while/body/eval_jaxpr/ppermute | solution.py:12
  124.1 3.7 %copy.75 = bf16[768,2048]{0,1:T(8,128)(2,1)} copy(bf16[768,2048]{0,1:T(8,128)(2,1)} %collective-permute-done) | data formatting | bytes 6291456 | tf_op jit(solution)/shard_map/while
  127.8 5.3 %collective-permute-start = (bf16[768,2048]{0,1:T(8,128)(2,1)}, bf16[768,2048]{0,1:T(8,128)(2,1)}, u32[]{:S(2)}, u32[]{:S(2)}) collective-permute-start(bf16[768,2048]{0,1:T(8,128)(2,1)} %get-tuple-element.274), channel_id=1, source_target_pairs={{0,1},{1,2},{2,3},{3,4},{4,5},{5,6},{6,7},{7,8},{8,9},{9,10},{10,1... | collective-permute-start | bytes 9437192 | tf_op jit(solution)/shard_map/while/body/eval_jaxpr/ppermute | solution.py:12
  135.0 32.6 %collective-permute-done = bf16[768,2048]{0,1:T(8,128)(2,1)} collective-permute-done((bf16[768,2048]{0,1:T(8,128)(2,1)}, bf16[768,2048]{0,1:T(8,128)(2,1)}, u32[]{:S(2)}, u32[]{:S(2)}) %collective-permute-start) | collective-permute-done | bytes 3145760 | tf_op jit(solution)/shard_map/while/body/eval_jaxpr/ppermute | solution.py:12
  167.6 3.7 %copy.75 = bf16[768,2048]{0,1:T(8,128)(2,1)} copy(bf16[768,2048]{0,1:T(8,128)(2,1)} %collective-permute-done) | data formatting | bytes 6291456 | tf_op jit(solution)/shard_map/while
  171.3 3.5 %copy.48 = f32[768,8,128]{0,2,1:T(8,128)} copy(f32[768,8,128]{2,0,1:T(8,128)} %get-tuple-element.178) | data formatting | bytes 6291456 | tf_op jit(solution)/shard_map/while | solution.py:85
  174.9 2.4 multiply_reduce_fusion.1
  178.3 2.8 %copy.60 = bf16[768,1024]{0,1:T(8,128)(2,1)} copy(bf16[768,1024]{1,0:T(8,128)(2,1)} %get-tuple-element.216) | data formatting | bytes 3145728
  182.9 3.2 %fusion.12 = bf16[768,1024]{0,1:T(8,128)(2,1)S(1)} fusion(f32[768,8,128]{0,2,1:T(8,128)} %copy.48, bf16[768,1024]{0,1:T(8,128)(2,1)} %copy.60, f32[1024]{0:T(1024)S(1)} %copy-done.6, f32[768]{0:T(1024)S(1)} %add_rsqrt_fusion, f32[768]{0:T(1024)S(1)} %broadcast_multiply_fusion, f32[768]{0:T(1024)S(1)} %copy-done.5), kind=kLoop, calls=%fused_computation.16 | loop fusion | flops 5505024 | bytes 6304768 | tf_op jit(solution)/shard_map/convert_element_type | solution.py:93
  191.9 52.7 %all-to-all-start = ((bf16[16,2,512]{2,1,0:T(2,128)(2,1)}), bf16[16,2,512]{2,1,0:T(2,128)(2,1)S(1)}, u32[]{:S(2)}, u32[]{:S(2)}) async-start(bf16[16,2,512]{2,1,0:T(2,128)(2,1)} %reshape.144), calls=%async_computation | async-start | bytes 65536 | tf_op jit(solution)/shard_map/all_to_all | solution.py:103
  244.6 4.9 %all-to-all-done = bf16[16,2,512]{2,1,0:T(2,128)(2,1)S(1)} async-done(((bf16[16,2,512]{2,1,0:T(2,128)(2,1)}), bf16[16,2,512]{2,1,0:T(2,128)(2,1)S(1)}, u32[]{:S(2)}, u32[]{:S(2)}) %all-to-all-start) | async-done | bytes 32800 | tf_op jit(solution)/shard_map/all_to_all | solution.py:103
  249.9 2.3 fusion.18
  (72 shorter events, 17.6 us)
Async XLA Ops:
  0.6 185.5 %copy-start = (bf16[1024,1024]{1,0:T(8,128)(2,1)S(1)}, bf16[1024,1024]{1,0:T(8,128)(2,1)}, u32[]{:S(2)}) copy-start(bf16[1024,1024]{1,0:T(8,128)(2,1)} %param.19) | copy-start | bytes 6291460
  0.6 8.1 %slice-start = ((s8[6291456]{0:T(1024)(128)(4,1)}), s8[4194304]{0:T(1024)(128)(4,1)S(1)}, s32[]{:S(2)}) async-start(s8[6291456]{0:T(1024)(128)(4,1)} %bitcast.52), calls=%async_computation.1 | async-start | bytes 8388608
  2.3 6.5 %slice-start.1 = ((s8[6291456]{0:T(1024)(128)(4,1)}), s8[2097152]{0:T(1024)(128)(4,1)S(1)}, s32[]{:S(2)}) async-start(s8[6291456]{0:T(1024)(128)(4,1)} %bitcast.52), calls=%async_computation.2 | async-start | bytes 4194304
  8.7 1.9 copy-start.13
  11.0 15.1 %copy-start.2 = (s32[8]{0:T(128)}, s32[8]{0:T(128)S(1)}, u32[]{:S(2)}) copy-start(s32[8]{0:T(128)S(1)} %add_bitcast_fusion) | copy-start | bytes 100
  21.4 5.3 %copy-start.1 = (s32[8]{0:T(128)S(1)}, s32[8]{0:T(128)}, u32[]{:S(2)}) copy-start(s32[8]{0:T(128)} %param.21) | copy-start | bytes 100
  42.3 38.2 %collective-permute-start = (bf16[768,2048]{0,1:T(8,128)(2,1)}, bf16[768,2048]{0,1:T(8,128)(2,1)}, u32[]{:S(2)}, u32[]{:S(2)}) collective-permute-start(bf16[768,2048]{0,1:T(8,128)(2,1)} %get-tuple-element.274), channel_id=1, source_target_pairs={{0,1},{1,2},{2,3},{3,4},{4,5},{5,6},{6,7},{7,8},{8,9},{9,10},{10,1... | collective-permute-start | bytes 9437192 | tf_op jit(solution)/shard_map/while/body/eval_jaxpr/ppermute | solution.py:12
  84.3 39.8 %collective-permute-start = (bf16[768,2048]{0,1:T(8,128)(2,1)}, bf16[768,2048]{0,1:T(8,128)(2,1)}, u32[]{:S(2)}, u32[]{:S(2)}) collective-permute-start(bf16[768,2048]{0,1:T(8,128)(2,1)} %get-tuple-element.274), channel_id=1, source_target_pairs={{0,1},{1,2},{2,3},{3,4},{4,5},{5,6},{6,7},{7,8},{8,9},{9,10},{10,1... | collective-permute-start | bytes 9437192 | tf_op jit(solution)/shard_map/while/body/eval_jaxpr/ppermute | solution.py:12
  127.8 39.8 %collective-permute-start = (bf16[768,2048]{0,1:T(8,128)(2,1)}, bf16[768,2048]{0,1:T(8,128)(2,1)}, u32[]{:S(2)}, u32[]{:S(2)}) collective-permute-start(bf16[768,2048]{0,1:T(8,128)(2,1)} %get-tuple-element.274), channel_id=1, source_target_pairs={{0,1},{1,2},{2,3},{3,4},{4,5},{5,6},{6,7},{7,8},{8,9},{9,10},{10,1... | collective-permute-start | bytes 9437192 | tf_op jit(solution)/shard_map/while/body/eval_jaxpr/ppermute | solution.py:12
  171.3 3.5 %copy-start.5 = (f32[768]{0:T(1024)S(1)}, f32[768]{0:T(1024)}, u32[]{:S(2)}) copy-start(f32[768]{0:T(1024)} %fusion.29) | copy-start | bytes 9220
  174.9 2.8 %copy-start.4 = (f32[768,8,128]{2,0,1:T(8,128)S(1)}, f32[768,8,128]{2,0,1:T(8,128)}, u32[]{:S(2)}) copy-start(f32[768,8,128]{2,0,1:T(8,128)} %get-tuple-element.178) | copy-start | bytes 9437188
  177.7 4.0 %copy-start.15 = (pred[16]{0:T(512)(128)(4,1)S(1)}, pred[16]{0:T(512)(128)(4,1)}, u32[]{:S(2)}) copy-start(pred[16]{0:T(512)(128)(4,1)} %iota_compare_fusion.6) | copy-start | bytes 52
  177.7 5.2 %copy-start.6 = (f32[1024]{0:T(1024)S(1)}, f32[1024]{0:T(1024)}, u32[]{:S(2)}) copy-start(f32[1024]{0:T(1024)} %param.18) | copy-start | bytes 12292
  182.9 3.2 %copy-start.8 = (bf16[768,1024]{1,0:T(8,128)(2,1)S(1)}, bf16[768,1024]{1,0:T(8,128)(2,1)}, u32[]{:S(2)}) copy-start(bf16[768,1024]{1,0:T(8,128)(2,1)} %param.17) | copy-start | bytes 4718596
  186.1 58.4 %copy-start.3 = (s32[8]{0:T(128)S(1)}, s32[8]{0:T(128)}, u32[]{:S(2)}) copy-start(s32[8]{0:T(128)} %copy-done.2) | copy-start | bytes 100
  186.1 58.4 %copy-start.14 = (s32[128]{0:T(128)S(1)}, s32[128]{0:T(128)}, u32[]{:S(2)}) copy-start(s32[128]{0:T(128)} %param.23) | copy-start | bytes 1540
  186.1 63.7 %copy-start.9 = (bf16[128,2048]{1,0:T(8,128)(2,1)S(1)}, bf16[128,2048]{1,0:T(8,128)(2,1)}, u32[]{:S(2)}) copy-start(bf16[128,2048]{1,0:T(8,128)(2,1)} %param.25) | copy-start | bytes 1572868
  186.2 63.7 %copy-start.10 = (bf16[2048,128]{1,0:T(8,128)(2,1)S(1)}, bf16[2048,128]{1,0:T(8,128)(2,1)}, u32[]{:S(2)}) copy-start(bf16[2048,128]{1,0:T(8,128)(2,1)} %param.24) | copy-start | bytes 1572868
  186.2 63.7 %copy-start.11 = (f32[2048]{0:T(1024)S(1)}, f32[2048]{0:T(1024)}, u32[]{:S(2)}) copy-start(f32[2048]{0:T(1024)} %param.27) | copy-start | bytes 24580
  186.2 63.7 %copy-start.12 = (f32[2048]{0:T(1024)S(1)}, f32[2048]{0:T(1024)}, u32[]{:S(2)}) copy-start(f32[2048]{0:T(1024)} %param.26) | copy-start | bytes 24580
  188.0 1.1 copy-start.7
  191.9 57.7 %all-to-all-start = ((bf16[16,2,512]{2,1,0:T(2,128)(2,1)}), bf16[16,2,512]{2,1,0:T(2,128)(2,1)S(1)}, u32[]{:S(2)}, u32[]{:S(2)}) async-start(bf16[16,2,512]{2,1,0:T(2,128)(2,1)} %reshape.144), calls=%async_computation | async-start | bytes 65536 | tf_op jit(solution)/shard_map/all_to_all | solution.py:103
